TPU v7x, 768 devices: a whole 4x8x12 slice. The times are simulated.
768 devices in a mesh: ctx: 96 (over x, z, core), head: 8 (over y).
Axes of the slice: x: 4, y: 8, z: 12, core: 2. Of those that a mesh axis runs over, the one named last changes fastest.
Arguments:
- queries: bfloat16 [24576, 4096], P('ctx', 'head'), may hold values from -64 to 64
- key_vectors: bfloat16 [24576, 1024], P('ctx', 'head'), may hold values from -4.5 to 4.5
- value_vectors: bfloat16 [24576, 1024], P('ctx', 'head'), may hold values from -6 to 6
- out_weight: bfloat16 [4096, 4096], P('head'), may hold values from -0.09375 to 0.09375
- offsets: int32 [25], replicated, may hold values from 0 to 24576, as said below
Outputs:
- projected: bfloat16 [4096, 24576], P('head', 'ctx')
Inputs may be any that keep to these rules, and one draw needn't show every extreme that they name: offsets[0] = 0 and offsets[24] = 24576; offsets rise strictly; every document has 1 to 3840 tokens and one has exactly 3840.
All inputs are finite; a program needn't handle non-finite values.
Results may differ from a plain program's by a relative error of at most 0.014.
Values may be sent and summed in bfloat16 or wider, within the bound.
A program may use at most 32 MiB of HBM per device.

v0:
```python
import jax
import jax.numpy as jnp
from jax import lax
from jax.sharding import PartitionSpec as P

HEAD_DIM = 128
SPAN = 16


masked_score = -1e30


def shifted(block, axis, distance):
    devices = range(lax.axis_size(axis))
    route = [(i - distance, i) for i in devices if i - distance in devices]
    return lax.ppermute(block, axis, route)


def doc_index(positions, offsets):
    boundaries = offsets[1:-1]
    return jnp.sum((positions[:, None] >= boundaries[None, :]).astype(jnp.int32), axis=1)


def attend(running, query_head_rows, kv_block, key_start, query_pos, query_doc, offsets):
    key_count = kv_block.shape[1]
    kv_groups = query_head_rows.shape[1]
    head_size = query_head_rows.shape[3]
    logit_scale = head_size ** (-0.5)
    key_pos = key_start + jnp.arange(key_count, dtype=jnp.int32)
    key_doc = doc_index(key_pos, offsets)
    visible = (
        (key_pos[None, :] >= 0)
        & (key_pos[None, :] <= query_pos[:, None])
        & (key_doc[None, :] == query_doc[:, None])
    )
    row_max, row_sum, weighted_values = running
    grouped_key_heads = kv_block[0].reshape(key_count, kv_groups, head_size)
    value_heads = kv_block[1].reshape(key_count, kv_groups, head_size)
    attention_logits = (
        jnp.einsum(
            "myqe,cye->yqmc", query_head_rows, grouped_key_heads, preferred_element_type=jnp.float32
        )
        * logit_scale
    )
    attention_logits = jnp.where(visible, attention_logits, masked_score)
    new_max = jnp.maximum(row_max, jnp.max(attention_logits, axis=-1))
    attention_probs = jnp.where(visible, jnp.exp(attention_logits - new_max[..., None]), 0.0)
    rescale = jnp.exp(row_max - new_max)
    row_sum = row_sum * rescale + jnp.sum(attention_probs, axis=-1)
    added = jnp.einsum(
        "avmk,kab->mavb",
        attention_probs.astype(jnp.bfloat16),
        value_heads,
        preferred_element_type=jnp.float32,
    )
    weighted_values = weighted_values * jnp.transpose(rescale, (2, 0, 1))[..., None] + added
    return (new_max, row_sum, weighted_values)


def on_device(queries, key_vectors, value_vectors, out_weight, offsets):
    row_count = queries.shape[0]
    kv_groups = key_vectors.shape[1] // HEAD_DIM
    group_size = queries.shape[1] // key_vectors.shape[1]
    position = lax.axis_index("ctx")
    first_row = position * row_count
    query_pos = first_row + jnp.arange(row_count, dtype=jnp.int32)
    query_doc = doc_index(query_pos, offsets)
    query_head_rows = queries.reshape(row_count, kv_groups, group_size, HEAD_DIM)
    kv_pair = jnp.stack([key_vectors, value_vectors])
    empty_max = jnp.full((kv_groups, group_size, row_count), masked_score, jnp.float32)
    empty_sum = jnp.zeros((kv_groups, group_size, row_count), jnp.float32)
    empty_weighted = jnp.zeros((row_count, kv_groups, group_size, HEAD_DIM), jnp.float32)
    running = (empty_max, empty_sum, empty_weighted)
    reach_steps = min(SPAN - 1, lax.axis_size("ctx") - 1)
    running = attend(running, query_head_rows, kv_pair, first_row, query_pos, query_doc, offsets)

    def advance(step_index, current):
        totals, moving = current
        moving = shifted(moving, "ctx", 1)
        totals = attend(
            totals,
            query_head_rows,
            moving,
            first_row - step_index * row_count,
            query_pos,
            query_doc,
            offsets,
        )
        return (totals, moving)

    running, leftover = lax.fori_loop(1, reach_steps + 1, advance, (running, kv_pair))
    row_max, row_sum, weighted_values = running
    attended = weighted_values / jnp.transpose(row_sum, (2, 0, 1))[..., None]
    attended = attended.reshape(row_count, kv_groups * group_size * HEAD_DIM).astype(jnp.bfloat16)
    return lax.psum_scatter(
        lax.dot_general(
            out_weight, attended, (((0,), (1,)), ((), ())), preferred_element_type=jnp.float32
        ).astype(jnp.bfloat16),
        "head",
        scatter_dimension=0,
        tiled=True,
    )


def solution(mesh):
    placed = (P("ctx", "head"), P("ctx", "head"), P("ctx", "head"), P("head", None), P())
    return jax.shard_map(
        on_device, mesh=mesh, in_specs=placed, out_specs=P("head", "ctx"), check_vma=False
    )
```

profile of v0, /device:TPU:1, one launch (start us, length us, event | category | flops | bytes accessed | tf_op | source)
XLA Modules:
  0.0 214.6 jit_solution(13421084536268908926)
XLA Ops:
  11.8 115.2 %while.21 = (s32[]{:T(128)}, f32[1,4,256]{2,1,0:T(4,128)S(1)}, f32[1,4,256]{2,1,0:T(4,128)S(1)}, f32[256,1,4,128]{3,0,2,1:T(8,128)S(1)}, bf16[2,256,128]{2,1,0:T...) while((s32[]{:T(128)}, f32[1,4,256]{2,1,0:T(4,128)S(1)}, ...), condition=%wide.region_7.0_spmd.clone.clone, body=%wide.region_3.7_spmd.clone.clone.sunk | while | flops 137122816 | bytes 5710797 | solution.py:91
  11.8 5.4 %collective-permute-start = (bf16[2,256,128]{2,1,0:T(8,128)(2,1)S(1)}, bf16[2,256,128]{2,1,0:T(8,128)(2,1)S(1)}, u32[]{:S(2)}, u32[]{:S(2)}) collective-permute-start(bf16[2,256,128]{2,1,0:T(8,128)(2,1)S(1)} %get-tuple-element.352), channel_id=1, source_target_pairs={{0,8},{8,16},{16,24},{24,32},{32,40},{40,48},{48,56},{56,64},{64,7... | collective-permute-start | bytes 393224 | tf_op jit(solution)/shard_map/while/body/eval_jaxpr/ppermute | solution.py:16
  17.5 6.8 %collective-permute-done = bf16[2,256,128]{2,1,0:T(8,128)(2,1)S(1)} collective-permute-done((bf16[2,256,128]{2,1,0:T(8,128)(2,1)S(1)}, bf16[2,256,128]{2,1,0:T(8,128)(2,1)S(1)}, u32[]{:S(2)}, u32[]{:S(2)}) %collective-permute-start) | collective-permute-done | bytes 131104 | tf_op jit(solution)/shard_map/while/body/eval_jaxpr/ppermute | solution.py:16
  25.5 1.9 collective-permute-start
  27.8 1.6 collective-permute-done
  30.5 4.4 %collective-permute-start = (bf16[2,256,128]{2,1,0:T(8,128)(2,1)S(1)}, bf16[2,256,128]{2,1,0:T(8,128)(2,1)S(1)}, u32[]{:S(2)}, u32[]{:S(2)}) collective-permute-start(bf16[2,256,128]{2,1,0:T(8,128)(2,1)S(1)} %get-tuple-element.352), channel_id=1, source_target_pairs={{0,8},{8,16},{16,24},{24,32},{32,40},{40,48},{48,56},{56,64},{64,7... | collective-permute-start | bytes 393224 | tf_op jit(solution)/shard_map/while/body/eval_jaxpr/ppermute | solution.py:16
  35.2 1.6 collective-permute-done
  37.9 4.4 %collective-permute-start = (bf16[2,256,128]{2,1,0:T(8,128)(2,1)S(1)}, bf16[2,256,128]{2,1,0:T(8,128)(2,1)S(1)}, u32[]{:S(2)}, u32[]{:S(2)}) collective-permute-start(bf16[2,256,128]{2,1,0:T(8,128)(2,1)S(1)} %get-tuple-element.352), channel_id=1, source_target_pairs={{0,8},{8,16},{16,24},{24,32},{32,40},{40,48},{48,56},{56,64},{64,7... | collective-permute-start | bytes 393224 | tf_op jit(solution)/shard_map/while/body/eval_jaxpr/ppermute | solution.py:16
  42.6 1.6 collective-permute-done
  45.3 4.4 %collective-permute-start = (bf16[2,256,128]{2,1,0:T(8,128)(2,1)S(1)}, bf16[2,256,128]{2,1,0:T(8,128)(2,1)S(1)}, u32[]{:S(2)}, u32[]{:S(2)}) collective-permute-start(bf16[2,256,128]{2,1,0:T(8,128)(2,1)S(1)} %get-tuple-element.352), channel_id=1, source_target_pairs={{0,8},{8,16},{16,24},{24,32},{32,40},{40,48},{48,56},{56,64},{64,7... | collective-permute-start | bytes 393224 | tf_op jit(solution)/shard_map/while/body/eval_jaxpr/ppermute | solution.py:16
  50.1 1.6 collective-permute-done
  52.7 4.4 %collective-permute-start = (bf16[2,256,128]{2,1,0:T(8,128)(2,1)S(1)}, bf16[2,256,128]{2,1,0:T(8,128)(2,1)S(1)}, u32[]{:S(2)}, u32[]{:S(2)}) collective-permute-start(bf16[2,256,128]{2,1,0:T(8,128)(2,1)S(1)} %get-tuple-element.352), channel_id=1, source_target_pairs={{0,8},{8,16},{16,24},{24,32},{32,40},{40,48},{48,56},{56,64},{64,7... | collective-permute-start | bytes 393224 | tf_op jit(solution)/shard_map/while/body/eval_jaxpr/ppermute | solution.py:16
  60.2 4.4 %collective-permute-start = (bf16[2,256,128]{2,1,0:T(8,128)(2,1)S(1)}, bf16[2,256,128]{2,1,0:T(8,128)(2,1)S(1)}, u32[]{:S(2)}, u32[]{:S(2)}) collective-permute-start(bf16[2,256,128]{2,1,0:T(8,128)(2,1)S(1)} %get-tuple-element.352), channel_id=1, source_target_pairs={{0,8},{8,16},{16,24},{24,32},{32,40},{40,48},{48,56},{56,64},{64,7... | collective-permute-start | bytes 393224 | tf_op jit(solution)/shard_map/while/body/eval_jaxpr/ppermute | solution.py:16
  67.6 4.4 %collective-permute-start = (bf16[2,256,128]{2,1,0:T(8,128)(2,1)S(1)}, bf16[2,256,128]{2,1,0:T(8,128)(2,1)S(1)}, u32[]{:S(2)}, u32[]{:S(2)}) collective-permute-start(bf16[2,256,128]{2,1,0:T(8,128)(2,1)S(1)} %get-tuple-element.352), channel_id=1, source_target_pairs={{0,8},{8,16},{16,24},{24,32},{32,40},{40,48},{48,56},{56,64},{64,7... | collective-permute-start | bytes 393224 | tf_op jit(solution)/shard_map/while/body/eval_jaxpr/ppermute | solution.py:16
  75.0 4.4 %collective-permute-start = (bf16[2,256,128]{2,1,0:T(8,128)(2,1)S(1)}, bf16[2,256,128]{2,1,0:T(8,128)(2,1)S(1)}, u32[]{:S(2)}, u32[]{:S(2)}) collective-permute-start(bf16[2,256,128]{2,1,0:T(8,128)(2,1)S(1)} %get-tuple-element.352), channel_id=1, source_target_pairs={{0,8},{8,16},{16,24},{24,32},{32,40},{40,48},{48,56},{56,64},{64,7... | collective-permute-start | bytes 393224 | tf_op jit(solution)/shard_map/while/body/eval_jaxpr/ppermute | solution.py:16
  82.4 4.4 %collective-permute-start = (bf16[2,256,128]{2,1,0:T(8,128)(2,1)S(1)}, bf16[2,256,128]{2,1,0:T(8,128)(2,1)S(1)}, u32[]{:S(2)}, u32[]{:S(2)}) collective-permute-start(bf16[2,256,128]{2,1,0:T(8,128)(2,1)S(1)} %get-tuple-element.352), channel_id=1, source_target_pairs={{0,8},{8,16},{16,24},{24,32},{32,40},{40,48},{48,56},{56,64},{64,7... | collective-permute-start | bytes 393224 | tf_op jit(solution)/shard_map/while/body/eval_jaxpr/ppermute | solution.py:16
  89.8 4.4 %collective-permute-start = (bf16[2,256,128]{2,1,0:T(8,128)(2,1)S(1)}, bf16[2,256,128]{2,1,0:T(8,128)(2,1)S(1)}, u32[]{:S(2)}, u32[]{:S(2)}) collective-permute-start(bf16[2,256,128]{2,1,0:T(8,128)(2,1)S(1)} %get-tuple-element.352), channel_id=1, source_target_pairs={{0,8},{8,16},{16,24},{24,32},{32,40},{40,48},{48,56},{56,64},{64,7... | collective-permute-start | bytes 393224 | tf_op jit(solution)/shard_map/while/body/eval_jaxpr/ppermute | solution.py:16
  97.3 4.4 %collective-permute-start = (bf16[2,256,128]{2,1,0:T(8,128)(2,1)S(1)}, bf16[2,256,128]{2,1,0:T(8,128)(2,1)S(1)}, u32[]{:S(2)}, u32[]{:S(2)}) collective-permute-start(bf16[2,256,128]{2,1,0:T(8,128)(2,1)S(1)} %get-tuple-element.352), channel_id=1, source_target_pairs={{0,8},{8,16},{16,24},{24,32},{32,40},{40,48},{48,56},{56,64},{64,7... | collective-permute-start | bytes 393224 | tf_op jit(solution)/shard_map/while/body/eval_jaxpr/ppermute | solution.py:16
  104.7 4.4 %collective-permute-start = (bf16[2,256,128]{2,1,0:T(8,128)(2,1)S(1)}, bf16[2,256,128]{2,1,0:T(8,128)(2,1)S(1)}, u32[]{:S(2)}, u32[]{:S(2)}) collective-permute-start(bf16[2,256,128]{2,1,0:T(8,128)(2,1)S(1)} %get-tuple-element.352), channel_id=1, source_target_pairs={{0,8},{8,16},{16,24},{24,32},{32,40},{40,48},{48,56},{56,64},{64,7... | collective-permute-start | bytes 393224 | tf_op jit(solution)/shard_map/while/body/eval_jaxpr/ppermute | solution.py:16
  112.1 4.4 %collective-permute-start = (bf16[2,256,128]{2,1,0:T(8,128)(2,1)S(1)}, bf16[2,256,128]{2,1,0:T(8,128)(2,1)S(1)}, u32[]{:S(2)}, u32[]{:S(2)}) collective-permute-start(bf16[2,256,128]{2,1,0:T(8,128)(2,1)S(1)} %get-tuple-element.352), channel_id=1, source_target_pairs={{0,8},{8,16},{16,24},{24,32},{32,40},{40,48},{48,56},{56,64},{64,7... | collective-permute-start | bytes 393224 | tf_op jit(solution)/shard_map/while/body/eval_jaxpr/ppermute | solution.py:16
  119.5 4.4 %collective-permute-start = (bf16[2,256,128]{2,1,0:T(8,128)(2,1)S(1)}, bf16[2,256,128]{2,1,0:T(8,128)(2,1)S(1)}, u32[]{:S(2)}, u32[]{:S(2)}) collective-permute-start(bf16[2,256,128]{2,1,0:T(8,128)(2,1)S(1)} %get-tuple-element.352), channel_id=1, source_target_pairs={{0,8},{8,16},{16,24},{24,32},{32,40},{40,48},{48,56},{56,64},{64,7... | collective-permute-start | bytes 393224 | tf_op jit(solution)/shard_map/while/body/eval_jaxpr/ppermute | solution.py:16
  127.2 4.8 %fusion.15 = bf16[4096,256]{0,1:T(8,128)(2,1)} fusion(bf16[256,512]{0,1:T(8,128)(2,1)S(1)} %bitcast.115, bf16[512,4096]{1,0:T(8,128)(2,1)} %param.10), kind=kOutput, calls=%fused_computation.27 | convolution fusion | flops 1074790400 | bytes 6553600 | tf_op jit(solution)/shard_map/dot_general | solution.py:96
  132.0 73.9 %reduce-scatter.2.cloned.1.call-done = bf16[512,256]{0,1:T(8,128)(2,1)} async-done(((bf16[4096,256]{0,1:T(8,128)(2,1)}), bf16[512,256]{0,1:T(8,128)(2,1)}) %reduce-scatter.2.cloned.1.call-update) | async-done | bytes 262160 | tf_op jit(solution)/shard_map/reduce_scatter | solution.py:95
  205.9 1.8 copy.23
  (213 shorter events, 42.2 us)
Async XLA Ops:
  6.5 5.2 %copy-start.2 = (s32[25]{0:T(128)S(1)}, s32[25]{0:T(128)}, u32[]{:S(2)}) copy-start(s32[25]{0:T(128)} %param.11) | copy-start | bytes 304
  6.5 5.2 %copy-start = (bf16[256,128]{1,0:T(8,128)(2,1)S(1)}, bf16[256,128]{1,0:T(8,128)(2,1)}, u32[]{:S(2)}) copy-start(bf16[256,128]{1,0:T(8,128)(2,1)} %param.8) | copy-start | bytes 196612
  6.5 5.2 %copy-start.1 = (bf16[256,128]{1,0:T(8,128)(2,1)S(1)}, bf16[256,128]{1,0:T(8,128)(2,1)}, u32[]{:S(2)}) copy-start(bf16[256,128]{1,0:T(8,128)(2,1)} %param.9) | copy-start | bytes 196612
  6.5 199.4 %reduce-scatter.2.cloned.1.call-start = ((), (), s32[]{:S(2)}) async-start(), calls=%async_computation.1 | async-start | bytes 2359296 | tf_op jit(solution)/shard_map/reduce_scatter | solution.py:95
  11.8 12.6 %collective-permute-start = (bf16[2,256,128]{2,1,0:T(8,128)(2,1)S(1)}, bf16[2,256,128]{2,1,0:T(8,128)(2,1)S(1)}, u32[]{:S(2)}, u32[]{:S(2)}) collective-permute-start(bf16[2,256,128]{2,1,0:T(8,128)(2,1)S(1)} %get-tuple-element.352), channel_id=1, source_target_pairs={{0,8},{8,16},{16,24},{24,32},{32,40},{40,48},{48,56},{56,64},{64,7... | collective-permute-start | bytes 393224 | tf_op jit(solution)/shard_map/while/body/eval_jaxpr/ppermute | solution.py:16
  25.5 3.9 %collective-permute-start = (bf16[2,256,128]{2,1,0:T(8,128)(2,1)S(1)}, bf16[2,256,128]{2,1,0:T(8,128)(2,1)S(1)}, u32[]{:S(2)}, u32[]{:S(2)}) collective-permute-start(bf16[2,256,128]{2,1,0:T(8,128)(2,1)S(1)} %get-tuple-element.352), channel_id=1, source_target_pairs={{0,8},{8,16},{16,24},{24,32},{32,40},{40,48},{48,56},{56,64},{64,7... | collective-permute-start | bytes 393224 | tf_op jit(solution)/shard_map/while/body/eval_jaxpr/ppermute | solution.py:16
  30.5 6.3 %collective-permute-start = (bf16[2,256,128]{2,1,0:T(8,128)(2,1)S(1)}, bf16[2,256,128]{2,1,0:T(8,128)(2,1)S(1)}, u32[]{:S(2)}, u32[]{:S(2)}) collective-permute-start(bf16[2,256,128]{2,1,0:T(8,128)(2,1)S(1)} %get-tuple-element.352), channel_id=1, source_target_pairs={{0,8},{8,16},{16,24},{24,32},{32,40},{40,48},{48,56},{56,64},{64,7... | collective-permute-start | bytes 393224 | tf_op jit(solution)/shard_map/while/body/eval_jaxpr/ppermute | solution.py:16
  37.9 6.3 %collective-permute-start = (bf16[2,256,128]{2,1,0:T(8,128)(2,1)S(1)}, bf16[2,256,128]{2,1,0:T(8,128)(2,1)S(1)}, u32[]{:S(2)}, u32[]{:S(2)}) collective-permute-start(bf16[2,256,128]{2,1,0:T(8,128)(2,1)S(1)} %get-tuple-element.352), channel_id=1, source_target_pairs={{0,8},{8,16},{16,24},{24,32},{32,40},{40,48},{48,56},{56,64},{64,7... | collective-permute-start | bytes 393224 | tf_op jit(solution)/shard_map/while/body/eval_jaxpr/ppermute | solution.py:16
  45.3 6.3 %collective-permute-start = (bf16[2,256,128]{2,1,0:T(8,128)(2,1)S(1)}, bf16[2,256,128]{2,1,0:T(8,128)(2,1)S(1)}, u32[]{:S(2)}, u32[]{:S(2)}) collective-permute-start(bf16[2,256,128]{2,1,0:T(8,128)(2,1)S(1)} %get-tuple-element.352), channel_id=1, source_target_pairs={{0,8},{8,16},{16,24},{24,32},{32,40},{40,48},{48,56},{56,64},{64,7... | collective-permute-start | bytes 393224 | tf_op jit(solution)/shard_map/while/body/eval_jaxpr/ppermute | solution.py:16
  52.7 6.3 %collective-permute-start = (bf16[2,256,128]{2,1,0:T(8,128)(2,1)S(1)}, bf16[2,256,128]{2,1,0:T(8,128)(2,1)S(1)}, u32[]{:S(2)}, u32[]{:S(2)}) collective-permute-start(bf16[2,256,128]{2,1,0:T(8,128)(2,1)S(1)} %get-tuple-element.352), channel_id=1, source_target_pairs={{0,8},{8,16},{16,24},{24,32},{32,40},{40,48},{48,56},{56,64},{64,7... | collective-permute-start | bytes 393224 | tf_op jit(solution)/shard_map/while/body/eval_jaxpr/ppermute | solution.py:16
  60.2 6.3 %collective-permute-start = (bf16[2,256,128]{2,1,0:T(8,128)(2,1)S(1)}, bf16[2,256,128]{2,1,0:T(8,128)(2,1)S(1)}, u32[]{:S(2)}, u32[]{:S(2)}) collective-permute-start(bf16[2,256,128]{2,1,0:T(8,128)(2,1)S(1)} %get-tuple-element.352), channel_id=1, source_target_pairs={{0,8},{8,16},{16,24},{24,32},{32,40},{40,48},{48,56},{56,64},{64,7... | collective-permute-start | bytes 393224 | tf_op jit(solution)/shard_map/while/body/eval_jaxpr/ppermute | solution.py:16
  67.6 6.3 %collective-permute-start = (bf16[2,256,128]{2,1,0:T(8,128)(2,1)S(1)}, bf16[2,256,128]{2,1,0:T(8,128)(2,1)S(1)}, u32[]{:S(2)}, u32[]{:S(2)}) collective-permute-start(bf16[2,256,128]{2,1,0:T(8,128)(2,1)S(1)} %get-tuple-element.352), channel_id=1, source_target_pairs={{0,8},{8,16},{16,24},{24,32},{32,40},{40,48},{48,56},{56,64},{64,7... | collective-permute-start | bytes 393224 | tf_op jit(solution)/shard_map/while/body/eval_jaxpr/ppermute | solution.py:16
  75.0 6.3 %collective-permute-start = (bf16[2,256,128]{2,1,0:T(8,128)(2,1)S(1)}, bf16[2,256,128]{2,1,0:T(8,128)(2,1)S(1)}, u32[]{:S(2)}, u32[]{:S(2)}) collective-permute-start(bf16[2,256,128]{2,1,0:T(8,128)(2,1)S(1)} %get-tuple-element.352), channel_id=1, source_target_pairs={{0,8},{8,16},{16,24},{24,32},{32,40},{40,48},{48,56},{56,64},{64,7... | collective-permute-start | bytes 393224 | tf_op jit(solution)/shard_map/while/body/eval_jaxpr/ppermute | solution.py:16
  82.4 6.3 %collective-permute-start = (bf16[2,256,128]{2,1,0:T(8,128)(2,1)S(1)}, bf16[2,256,128]{2,1,0:T(8,128)(2,1)S(1)}, u32[]{:S(2)}, u32[]{:S(2)}) collective-permute-start(bf16[2,256,128]{2,1,0:T(8,128)(2,1)S(1)} %get-tuple-element.352), channel_id=1, source_target_pairs={{0,8},{8,16},{16,24},{24,32},{32,40},{40,48},{48,56},{56,64},{64,7... | collective-permute-start | bytes 393224 | tf_op jit(solution)/shard_map/while/body/eval_jaxpr/ppermute | solution.py:16
  89.8 6.3 %collective-permute-start = (bf16[2,256,128]{2,1,0:T(8,128)(2,1)S(1)}, bf16[2,256,128]{2,1,0:T(8,128)(2,1)S(1)}, u32[]{:S(2)}, u32[]{:S(2)}) collective-permute-start(bf16[2,256,128]{2,1,0:T(8,128)(2,1)S(1)} %get-tuple-element.352), channel_id=1, source_target_pairs={{0,8},{8,16},{16,24},{24,32},{32,40},{40,48},{48,56},{56,64},{64,7... | collective-permute-start | bytes 393224 | tf_op jit(solution)/shard_map/while/body/eval_jaxpr/ppermute | solution.py:16
  97.3 6.3 %collective-permute-start = (bf16[2,256,128]{2,1,0:T(8,128)(2,1)S(1)}, bf16[2,256,128]{2,1,0:T(8,128)(2,1)S(1)}, u32[]{:S(2)}, u32[]{:S(2)}) collective-permute-start(bf16[2,256,128]{2,1,0:T(8,128)(2,1)S(1)} %get-tuple-element.352), channel_id=1, source_target_pairs={{0,8},{8,16},{16,24},{24,32},{32,40},{40,48},{48,56},{56,64},{64,7... | collective-permute-start | bytes 393224 | tf_op jit(solution)/shard_map/while/body/eval_jaxpr/ppermute | solution.py:16
  104.7 6.3 %collective-permute-start = (bf16[2,256,128]{2,1,0:T(8,128)(2,1)S(1)}, bf16[2,256,128]{2,1,0:T(8,128)(2,1)S(1)}, u32[]{:S(2)}, u32[]{:S(2)}) collective-permute-start(bf16[2,256,128]{2,1,0:T(8,128)(2,1)S(1)} %get-tuple-element.352), channel_id=1, source_target_pairs={{0,8},{8,16},{16,24},{24,32},{32,40},{40,48},{48,56},{56,64},{64,7... | collective-permute-start | bytes 393224 | tf_op jit(solution)/shard_map/while/body/eval_jaxpr/ppermute | solution.py:16
  112.1 6.3 %collective-permute-start = (bf16[2,256,128]{2,1,0:T(8,128)(2,1)S(1)}, bf16[2,256,128]{2,1,0:T(8,128)(2,1)S(1)}, u32[]{:S(2)}, u32[]{:S(2)}) collective-permute-start(bf16[2,256,128]{2,1,0:T(8,128)(2,1)S(1)} %get-tuple-element.352), channel_id=1, source_target_pairs={{0,8},{8,16},{16,24},{24,32},{32,40},{40,48},{48,56},{56,64},{64,7... | collective-permute-start | bytes 393224 | tf_op jit(solution)/shard_map/while/body/eval_jaxpr/ppermute | solution.py:16
  119.5 6.3 %collective-permute-start = (bf16[2,256,128]{2,1,0:T(8,128)(2,1)S(1)}, bf16[2,256,128]{2,1,0:T(8,128)(2,1)S(1)}, u32[]{:S(2)}, u32[]{:S(2)}) collective-permute-start(bf16[2,256,128]{2,1,0:T(8,128)(2,1)S(1)} %get-tuple-element.352), channel_id=1, source_target_pairs={{0,8},{8,16},{16,24},{24,32},{32,40},{40,48},{48,56},{56,64},{64,7... | collective-permute-start | bytes 393224 | tf_op jit(solution)/shard_map/while/body/eval_jaxpr/ppermute | solution.py:16
Sparse Core Ops, SparseCore 0:
  132.1 73.7 reduce-scatter.1
where the time goes:
time: 219 us; the launch traced here: 215 us
  waiting for transfers between devices  102 us (47%)
  starting transfers between devices  63.9 us (29%)
  matrix products  19.9 us (9%)
  between operations  13.5 us (6%)
  other arithmetic  8.15 us (4%)
  local copies, waits for them, and re-layouts  5.3 us (2%)
    reduce_scatter x1, waiting for transfers between devices, on_device(): lax.psum_scatter(lax.dot_general(out_weight, attended, (((0,), (1,)), (()...  73.9 us
    ppermute x15, starting transfers between devices, shifted(): return lax.ppermute(block, axis, route)  63.9 us
    ppermute x15, waiting for transfers between devices, shifted(): return lax.ppermute(block, axis, route)  28.5 us
    dot_general x16, matrix products, attend(): jnp.einsum('avmk,kab->mavb', attention_probs.astype(jnp.bfloat16), value_...  8.93 us
    dot_general x16, matrix products, attend(): jnp.einsum('myqe,cye->yqmc', query_head_rows, grouped_key_heads, preferre...  6.13 us
    dot_general x1, matrix products, on_device(): lax.dot_general(out_weight, attended, (((0,), (1,)), ((), ())), preferred...  4.82 us
  transfers between devices with their start and end apart: 16, of which 16 were waited for; matrix products, arithmetic and copies ran while one was open for 2% of the time, Pallas kernels for 0%

commit v1 on v0

v1 whole, which is shorter than its diff:
```python
import functools
import math

import jax
import jax.numpy as jnp
from jax import lax
from jax.experimental import pallas as pl
from jax.experimental.pallas import tpu as pltpu
from jax.sharding import PartitionSpec as P

HEAD_DIM = 128
LAST = 7
MESH = pl.DeviceIdType.MESH
NEG = -1e30
UNSEEN = -(1 << 24)

CHAINS = ((4, 1, -1, 0), (4, -1, 1, 1), (5, 1, -1, 1), (3, -1, 1, 0))


def stops(chain):
    first, step, _, _ = CHAINS[chain]
    return [r % 8 for r in range(first, 8 if step == 1 else 0, step)]


def kernel(
    n_ctx, n_head, offsets_ref, q_hbm, k_hbm, v_hbm, w_hbm, out_ref,
    kv, q_ref, w_ref, bound, m_ref, l_ref, acc, att, part, sums, landed,
    in_sem, w_sem, hop_send, hop_recv, share_send, share_recv, last_send, last_recv,
    sum_send, sum_recv,
):
    ctx, head = lax.axis_index("ctx"), lax.axis_index("head")
    core = lax.rem(ctx, 2)
    other = 1 - core
    rows = q_ref.shape[0]
    heads = q_ref.shape[1] // HEAD_DIM
    half = rows // 2
    width = w_ref.shape[2]
    scale = math.log2(math.e) / math.sqrt(HEAD_DIM)
    after, before = lax.rem(ctx + 2, n_ctx), lax.rem(ctx + n_ctx - 2, n_ctx)
    partner = ctx + 1 - 2 * core
    across = lax.rem(ctx + n_ctx + 2 * core - 1, n_ctx)
    up, down = lax.rem(head + 1, n_head), lax.rem(head + n_head - 1, n_head)

    loads = [
        pltpu.make_async_copy(k_hbm, kv.at[0, core, 0], in_sem.at[0]),
        pltpu.make_async_copy(v_hbm, kv.at[0, core, 1], in_sem.at[1]),
        pltpu.make_async_copy(q_hbm, q_ref, in_sem.at[2]),
    ]
    for load in loads:
        load.start()

    def weight_load(r):
        first = pl.multiple_of(lax.rem(head + r, n_head) * width, width)
        return pltpu.make_async_copy(w_hbm.at[:, pl.ds(first, width)], w_ref.at[r], w_sem.at[r])

    for r in (4, 3, 5, 2, 6, 1, 7, 0):
        weight_load(r).start()

    barrier = pltpu.get_barrier_semaphore()
    for to in (
        (after, head), (before, head), (partner, head), (across, head), (ctx, up), (ctx, down)
    ):
        pl.semaphore_signal(barrier, inc=1, device_id=to, device_id_type=MESH)
    pl.semaphore_wait(barrier, 6)

    def hop(k, piece):
        return pltpu.make_async_remote_copy(
            src_ref=kv.at[k, core, piece],
            dst_ref=kv.at[k + 1, core, piece],
            send_sem=hop_send.at[k, piece],
            recv_sem=hop_recv.at[k, piece],
            device_id=(after, head),
            device_id_type=MESH,
        )

    def share(k, piece):
        return pltpu.make_async_remote_copy(
            src_ref=kv.at[k, core, piece],
            dst_ref=kv.at[k, core, piece],
            send_sem=share_send.at[k, piece],
            recv_sem=share_recv.at[k, piece],
            device_id=(partner, head),
            device_id_type=MESH,
        )

    def last(piece):
        return pltpu.make_async_remote_copy(
            src_ref=kv.at[LAST, 1, piece],
            dst_ref=kv.at[LAST + 1, 1, piece],
            send_sem=last_send.at[piece],
            recv_sem=last_recv.at[piece],
            device_id=(across, head),
            device_id_type=MESH,
        )

    def block(k, parity, first, diagonal=False):
        keys = kv[k, parity, 0]
        values = jnp.transpose(kv[k, parity, 1])
        lowest = bound[0:1, :] - first
        at = lax.broadcasted_iota(jnp.int32, (rows, rows), 0)
        seen = at >= lowest
        if diagonal:
            seen = seen & (at <= lax.broadcasted_iota(jnp.int32, (rows, rows), 1))
        for h in range(heads):
            cols = slice(h * HEAD_DIM, (h + 1) * HEAD_DIM)
            scores = lax.dot_general(
                keys, q_ref[:, cols], (((1,), (1,)), ((), ())), preferred_element_type=jnp.float32
            )
            scores = jnp.where(seen, scores, NEG)
            top = jnp.max(scores, axis=0, keepdims=True)
            if not diagonal:
                old = m_ref[h : h + 1, :]
                top = jnp.maximum(top, old)
            weights = jnp.exp2((scores - top) * scale)
            total = jnp.sum(weights, axis=0, keepdims=True)
            added = jnp.dot(values, weights.astype(jnp.bfloat16), preferred_element_type=jnp.float32)
            if not diagonal:
                fade = jnp.exp2((old - top) * scale)
                total = total + l_ref[h : h + 1, :] * fade
                added = added + acc[cols, :] * fade
            m_ref[h : h + 1, :] = top
            l_ref[h : h + 1, :] = total
            acc[cols, :] = added

    def base(k):
        return (ctx - core - 2 * k) * rows

    for piece in range(2):
        loads[piece].wait()
        hop(0, piece).start()
        share(0, piece).start()

    pos = ctx * rows + lax.broadcasted_iota(jnp.int32, (8, rows), 1)
    start = jnp.zeros((8, rows), jnp.int32)
    for j in range(1, offsets_ref.shape[0] - 1):
        edge = offsets_ref[j]
        start = jnp.maximum(start, jnp.where(pos >= edge, edge, 0))
    bound[...] = start

    loads[2].wait()
    block(0, core, ctx * rows, diagonal=True)

    def stage(k, forward):
        hop(k - 1, 0).wait_recv()
        forward(0)
        share(k, 0).start()
        share(k - 1, 0).wait_recv()
        share(k - 1, 1).wait_recv()
        first = base(k - 1) + other * rows
        block(k - 1, other, jnp.where(first > ctx * rows, UNSEEN, first))
        hop(k - 1, 1).wait_recv()
        forward(1)
        share(k, 1).start()
        block(k, core, base(k) + core * rows)

    def middle(k, carry):
        stage(k, lambda piece: hop(k, piece).start())
        return carry

    lax.fori_loop(1, LAST, middle, 0)

    def tail(piece):
        @pl.when(core == 1)
        def _():
            last(piece).start()

    stage(LAST, tail)
    share(LAST, 0).wait_recv()
    share(LAST, 1).wait_recv()
    block(LAST, other, base(LAST) + other * rows)

    @pl.when(core == 0)
    def _():
        last(0).wait_recv()
        last(1).wait_recv()
        block(LAST + 1, 1, base(LAST + 1) + rows)

    for h in range(heads):
        cols = slice(h * HEAD_DIM, (h + 1) * HEAD_DIM)
        att[:, cols] = jnp.transpose(acc[cols, :] / l_ref[h : h + 1, :]).astype(jnp.bfloat16)

    def send(chain, i):
        return pltpu.make_async_remote_copy(
            src_ref=sums.at[chain, i],
            dst_ref=landed.at[chain, i],
            send_sem=sum_send.at[chain, i],
            recv_sem=sum_recv.at[chain, i],
            device_id=(ctx, up if CHAINS[chain][2] == 1 else down),
            device_id_type=MESH,
        )

    def tokens(chain):
        return slice(CHAINS[chain][3] * half, (CHAINS[chain][3] + 1) * half)

    for r in (4, 5, 3, 6, 2, 7, 1, 0):
        weight_load(r).wait()
        share_of = jnp.dot(att[...], w_ref[r], preferred_element_type=jnp.float32)
        for chain in range(4):
            if stops(chain)[0] == r:
                sums[chain, 0] = share_of[tokens(chain), :].astype(jnp.bfloat16)
        part[r] = share_of
        for chain in range(4):
            if stops(chain)[0] == r:
                send(chain, 0).start()

    for i in range(4):
        for chain in range(4):
            order = stops(chain) + [0]
            if i + 1 >= len(order):
                continue
            send(chain, i).wait_recv()
            mine = part[order[i + 1], tokens(chain), :] + landed[chain, i].astype(jnp.float32)
            if order[i + 1] == 0:
                part[0, tokens(chain), :] = mine
            else:
                sums[chain, i + 1] = mine.astype(jnp.bfloat16)
                send(chain, i + 1).start()
    out_ref[...] = jnp.transpose(part[0]).astype(jnp.bfloat16)

    for chain in range(4):
        for i in range(len(stops(chain))):
            send(chain, i).wait_send()

    def drain(k, carry):
        for piece in range(2):
            share(k, piece).wait_send()

            @pl.when(k < LAST)
            def _():
                hop(k, piece).wait_send()

        return carry

    lax.fori_loop(0, LAST + 1, drain, 0)

    @pl.when(core == 1)
    def _():
        last(0).wait_send()
        last(1).wait_send()


def on_device(n_ctx, n_head, queries, key_vectors, value_vectors, out_weight, offsets):
    rows, columns = queries.shape
    depth, features = out_weight.shape
    width = features // n_head
    dma = pltpu.SemaphoreType.DMA
    return pl.pallas_call(
        functools.partial(kernel, n_ctx, n_head),
        out_shape=jax.ShapeDtypeStruct((width, rows), jnp.bfloat16),
        in_specs=[pl.BlockSpec(memory_space=pltpu.SMEM)] + [pl.BlockSpec(memory_space=pl.ANY)] * 4,
        out_specs=pl.BlockSpec(memory_space=pltpu.VMEM),
        scratch_shapes=[
            pltpu.VMEM((LAST + 2, 2, 2, rows, HEAD_DIM), jnp.bfloat16),
            pltpu.VMEM((rows, columns), jnp.bfloat16),
            pltpu.VMEM((n_head, depth, width), jnp.bfloat16),
            pltpu.VMEM((8, rows), jnp.int32),
            pltpu.VMEM((8, rows), jnp.float32),
            pltpu.VMEM((8, rows), jnp.float32),
            pltpu.VMEM((columns, rows), jnp.float32),
            pltpu.VMEM((rows, columns), jnp.bfloat16),
            pltpu.VMEM((n_head, rows, width), jnp.float32),
            pltpu.VMEM((4, 4, rows // 2, width), jnp.bfloat16),
            pltpu.VMEM((4, 4, rows // 2, width), jnp.bfloat16),
            dma((3,)),
            dma((n_head,)),
            dma((LAST, 2)),
            dma((LAST, 2)),
            dma((LAST + 1, 2)),
            dma((LAST + 1, 2)),
            dma((2,)),
            dma((2,)),
            dma((4, 4)),
            dma((4, 4)),
        ],
        compiler_params=pltpu.CompilerParams(
            collective_id=0, has_side_effects=True, vmem_limit_bytes=40 << 20
        ),
    )(offsets, queries, key_vectors, value_vectors, out_weight)


def solution(mesh):
    placed = (P("ctx", "head"), P("ctx", "head"), P("ctx", "head"), P("head", None), P())
    return jax.shard_map(
        functools.partial(on_device, mesh.shape["ctx"], mesh.shape["head"]),
        mesh=mesh,
        in_specs=placed,
        out_specs=P("head", "ctx"),
        check_vma=False,
    )
```

time: 219 us -> 77.9 us (0.36)
  the two profiles are of different devices: /device:TPU:1 before, /device:TPU:8 now
where the time goes in v1:
time: 77.9 us; the launch traced here: 77.6 us
  Pallas kernels  71.4 us (92%)
  local copies, waits for them, and re-layouts  6.17 us (8%)
    pallas_call x1, Pallas kernels, on_device(): pl.pallas_call(functools.partial(kernel, n_ctx, n_head), out_shape=jax.Sh...  71.4 us
    unnamed x11, local copies, waits for them, and re-layouts  6.17 us

profile of v1, /device:TPU:8, one launch (start us, length us, event | category | flops | bytes accessed | tf_op | source)
XLA Modules:
  0.0 77.6 jit_solution(10863678344252293461)
XLA Ops:
  0.0 0.0 copy-start
  0.0 2.2 %copy-done = bf16[512,4096]{1,0:T(8,128)(2,1)S(1)} copy-done((bf16[512,4096]{1,0:T(8,128)(2,1)S(1)}, bf16[512,4096]{1,0:T(8,128)(2,1)}, u32[]{:S(2)}) %copy-start) | copy-done | bytes 4194328
  2.2 0.0 copy-start.1
  2.2 0.9 %copy-done.1 = bf16[256,512]{1,0:T(8,128)(2,1)S(1)} copy-done((bf16[256,512]{1,0:T(8,128)(2,1)S(1)}, bf16[256,512]{1,0:T(8,128)(2,1)}, u32[]{:S(2)}) %copy-start.1) | copy-done | bytes 262168
  3.1 0.0 copy-start.2
  3.1 0.8 %copy-done.2 = bf16[256,128]{1,0:T(8,128)(2,1)S(1)} copy-done((bf16[256,128]{1,0:T(8,128)(2,1)S(1)}, bf16[256,128]{1,0:T(8,128)(2,1)}, u32[]{:S(2)}) %copy-start.2) | copy-done | bytes 65560
  4.0 0.0 copy-start.3
  4.0 0.8 %copy-done.3 = bf16[256,128]{1,0:T(8,128)(2,1)S(1)} copy-done((bf16[256,128]{1,0:T(8,128)(2,1)S(1)}, bf16[256,128]{1,0:T(8,128)(2,1)}, u32[]{:S(2)}) %copy-start.3) | copy-done | bytes 65560
  4.8 0.0 copy-start.4
  4.8 0.7 copy-done.4
  5.5 71.4 %shard_map.55 = bf16[512,256]{1,0:T(8,128)(2,1)S(1)} custom-call(s32[25]{0:T(128)S(1)} %copy-done.4, bf16[256,512]{1,0:T(8,128)(2,1)S(1)} %copy-done.1, bf16[256,128]{1,0:T(8,128)(2,1)S(1)} %copy-done.2, bf16[256,128]{1,0:T(8,128)(2,1)S(1)} %copy-done.3, bf16[512,4096]{1,0:T(8,128)(2,1)S(1)} %copy-done), custom_call_target="tpu_custom_call" | custom-call | tf_op jit(solution)/shard_map/pallas_call | solution.py:247
  76.9 0.7 copy.7
Async XLA Ops:
  0.0 2.2 %copy-start = (bf16[512,4096]{1,0:T(8,128)(2,1)S(1)}, bf16[512,4096]{1,0:T(8,128)(2,1)}, u32[]{:S(2)}) copy-start(bf16[512,4096]{1,0:T(8,128)(2,1)} %w_hbm.1) | copy-start | bytes 12582916
  2.2 0.9 %copy-start.1 = (bf16[256,512]{1,0:T(8,128)(2,1)S(1)}, bf16[256,512]{1,0:T(8,128)(2,1)}, u32[]{:S(2)}) copy-start(bf16[256,512]{1,0:T(8,128)(2,1)} %q_hbm.1) | copy-start | bytes 786436
  3.1 0.8 %copy-start.2 = (bf16[256,128]{1,0:T(8,128)(2,1)S(1)}, bf16[256,128]{1,0:T(8,128)(2,1)}, u32[]{:S(2)}) copy-start(bf16[256,128]{1,0:T(8,128)(2,1)} %k_hbm.1) | copy-start | bytes 196612
  4.0 0.8 %copy-start.3 = (bf16[256,128]{1,0:T(8,128)(2,1)S(1)}, bf16[256,128]{1,0:T(8,128)(2,1)}, u32[]{:S(2)}) copy-start(bf16[256,128]{1,0:T(8,128)(2,1)} %v_hbm.1) | copy-start | bytes 196612
  4.8 0.7 copy-start.4

commit v2 on v1

v2 whole, which is shorter than its diff:
```python
import functools
import math

import jax
import jax.numpy as jnp
from jax import lax
from jax.experimental import pallas as pl
from jax.experimental.pallas import tpu as pltpu
from jax.sharding import PartitionSpec as P

HEAD_DIM = 128
MESH = pl.DeviceIdType.MESH
NEG = -1e30
FAR = 1 << 24
BARRED = -float(1 << 17)

EDGES = (
    (0, 0, 2), (0, 2, 2), (0, 4, 2), (0, 2, -1), (0, 4, -1), (0, 6, -1), (0, 6, 1),
    (1, 0, 2), (1, 2, 2), (1, 2, -1), (1, 4, -1), (1, 0, 8), (1, 8, -2), (1, 6, 1), (1, 6, -1),
)
SHARED = (range(8), range(9))

CHAINS = ((4, 1, -1, 0), (4, -1, 1, 1), (5, 1, -1, 1), (3, -1, 1, 0))


def stops(chain):
    first, step, _, _ = CHAINS[chain]
    return [r % 8 for r in range(first, 8 if step == 1 else 0, step)]


def kernel(
    n_ctx, n_head, offsets_ref, q_hbm, k_hbm, v_hbm, w_hbm, out_ref,
    kv, q_ref, w_ref, edges, qm, m_ref, acc, att, part, sums, landed,
    in_sem, w_sem, hop_send, hop_recv, share_send, share_recv, last_send, last_recv,
    sum_send, sum_recv,
):
    ctx, head = lax.axis_index("ctx"), lax.axis_index("head")
    core = lax.rem(ctx, 2)
    other = 1 - core
    rows = q_ref.shape[0]
    heads = q_ref.shape[1] // HEAD_DIM
    half = rows // 2
    width = w_ref.shape[2]
    scale = math.log2(math.e) / math.sqrt(HEAD_DIM)
    partner = ctx + 1 - 2 * core
    across = lax.rem(ctx + n_ctx + 6 * core - 3, n_ctx)
    up, down = lax.rem(head + 1, n_head), lax.rem(head + n_head - 1, n_head)

    loads = [
        pltpu.make_async_copy(k_hbm, kv.at[0, core, 0], in_sem.at[0]),
        pltpu.make_async_copy(v_hbm, kv.at[0, core, 1], in_sem.at[1]),
        pltpu.make_async_copy(q_hbm, q_ref, in_sem.at[2]),
    ]
    for load in loads:
        load.start()

    def weight_load(r):
        first = pl.multiple_of(lax.rem(head + r, n_head) * width, width)
        return pltpu.make_async_copy(w_hbm.at[:, pl.ds(first, width)], w_ref.at[r], w_sem.at[r])

    for r in (4, 3, 5, 2, 6, 1, 7, 0):
        weight_load(r).start()

    barrier = pltpu.get_barrier_semaphore()
    for delta in (1, -1, 2, -2, 8, -8):
        near = lax.rem(ctx + n_ctx + 2 * delta, n_ctx)
        pl.semaphore_signal(barrier, inc=1, device_id=(near, head), device_id_type=MESH)
    for to in ((partner, head), (across, head), (ctx, up), (ctx, down)):
        pl.semaphore_signal(barrier, inc=1, device_id=to, device_id_type=MESH)
    pl.semaphore_wait(barrier, 10)

    def chip(delta):
        return lax.rem(ctx + n_ctx + 2 * delta, n_ctx)

    def edge(piece, slot, delta):
        return pltpu.make_async_remote_copy(
            src_ref=kv.at[slot, core, piece],
            dst_ref=kv.at[slot + delta, core, piece],
            send_sem=hop_send.at[piece, slot + delta],
            recv_sem=hop_recv.at[piece, slot + delta],
            device_id=(chip(delta), head),
            device_id_type=MESH,
        )

    def share(piece, slot):
        return pltpu.make_async_remote_copy(
            src_ref=kv.at[slot, core, piece],
            dst_ref=kv.at[slot, core, piece],
            send_sem=share_send.at[piece, slot],
            recv_sem=share_recv.at[piece, slot],
            device_id=(partner, head),
            device_id_type=MESH,
        )

    def last():
        return pltpu.make_async_remote_copy(
            src_ref=kv.at[6, 1, 0],
            dst_ref=kv.at[8, 1, 0],
            send_sem=last_send.at[0],
            recv_sem=last_recv.at[0],
            device_id=(across, head),
            device_id_type=MESH,
        )

    def first_of(slot, parity):
        return (ctx - core - 2 * slot + parity) * rows

    def block(slot, parity, first, diagonal=False):
        keys = kv[slot, parity, 0]
        values = jnp.transpose(kv[slot, parity, 1])
        at = first + lax.broadcasted_iota(jnp.int32, (rows, HEAD_DIM), 0)
        among = (at >= edges[0:1, :]) & (at < edges[8:9, :])
        keys = jnp.concatenate([keys, jnp.where(among, 1.0, 0.0).astype(jnp.bfloat16)], axis=1)
        values = jnp.concatenate([values, jnp.ones((16, rows), jnp.bfloat16)], axis=0)
        if diagonal:
            seen = lax.broadcasted_iota(jnp.int32, (rows, rows), 0) <= lax.broadcasted_iota(
                jnp.int32, (rows, rows), 1
            )

        def score(h):
            got = lax.dot_general(
                keys, qm[h], (((1,), (1,)), ((), ())), preferred_element_type=jnp.float32
            )
            return jnp.where(seen, got, NEG) if diagonal else got

        ready = score(0)
        for h in range(heads):
            scores = ready
            if h + 1 < heads:
                ready = score(h + 1)
            top = jnp.max(scores, axis=0, keepdims=True)
            if not diagonal:
                old = m_ref[h : h + 1, :]
                top = jnp.maximum(top, old)
            weights = jnp.exp2((scores - top) * scale).astype(jnp.bfloat16)
            added = jnp.dot(values, weights, preferred_element_type=jnp.float32)
            if not diagonal:
                added = added + acc[h] * jnp.exp2((old - top) * scale)
            m_ref[h : h + 1, :] = top
            acc[h] = added

    for piece in range(2):
        loads[piece].wait()
        edge(piece, 0, 2).start()
        share(piece, 0).start()
    edge(1, 0, 8).start()

    lane = lax.broadcasted_iota(jnp.int32, (8, HEAD_DIM), 1)
    low = jnp.full((8, HEAD_DIM), FAR, jnp.int32)
    high = low
    n_docs = offsets_ref.shape[0] - 1
    for j in range(n_docs):
        low = jnp.where(lane == j, offsets_ref[j], low)
        high = jnp.where(lane == j, offsets_ref[j + 1], high)
    low = jnp.where(lane == n_docs, -FAR, low)
    high = jnp.where(lane == n_docs, 0, high)
    edges[0:8, :] = low
    edges[8:16, :] = high

    at = ctx * rows + lax.broadcasted_iota(jnp.int32, (rows, HEAD_DIM), 0)
    among = (at >= edges[0:1, :]) & (at < edges[8:9, :])
    barred = jnp.where(among, 0.0, BARRED).astype(jnp.bfloat16)
    loads[2].wait()
    for h in range(heads):
        qm[h, :, 0:HEAD_DIM] = q_ref[:, h * HEAD_DIM : (h + 1) * HEAD_DIM]
        qm[h, :, HEAD_DIM : 2 * HEAD_DIM] = barred

    def mine(slot):
        block(slot, core, first_of(slot, core))

    def theirs(slot):
        share(0, slot).wait_recv()
        share(1, slot).wait_recv()
        block(slot, other, first_of(slot, other))

    def arrived(piece, slot, *deltas):
        edge(piece, slot, 0).wait_recv()
        for delta in deltas:
            edge(piece, slot, delta).start()
        share(piece, slot).start()

    block(0, core, first_of(0, core), diagonal=True)
    share(0, 0).wait_recv()
    share(1, 0).wait_recv()
    block(0, other, jnp.where(core == 0, -FAR // 2, first_of(0, other)))
    arrived(0, 2, 2, -1)
    arrived(1, 2, 2, -1)
    mine(2)
    arrived(1, 8, -2)
    theirs(2)
    arrived(0, 4, 2, -1)
    arrived(1, 4, -1)
    mine(4)
    arrived(0, 1)
    arrived(1, 1)
    mine(1)
    arrived(1, 6, 1, -1)
    theirs(4)
    arrived(0, 6, 1, -1)

    @pl.when(core == 1)
    def _():
        last().start()

    theirs(1)
    mine(6)
    arrived(0, 3)
    arrived(1, 3)
    mine(3)
    theirs(6)
    arrived(0, 5)
    arrived(1, 5)
    theirs(3)
    arrived(0, 7)
    arrived(1, 7)
    mine(5)
    mine(7)
    theirs(5)
    theirs(7)
    share(1, 8).wait_recv()

    @pl.when(core == 0)
    def _():
        last().wait_recv()
        block(8, 1, first_of(8, 1))

    for h in range(heads):
        cols = slice(h * HEAD_DIM, (h + 1) * HEAD_DIM)
        att[:, cols] = jnp.transpose(
            acc[h, 0:HEAD_DIM, :] / acc[h, HEAD_DIM : HEAD_DIM + 1, :]
        ).astype(jnp.bfloat16)

    def send(chain, i):
        return pltpu.make_async_remote_copy(
            src_ref=sums.at[chain, i],
            dst_ref=landed.at[chain, i],
            send_sem=sum_send.at[chain, i],
            recv_sem=sum_recv.at[chain, i],
            device_id=(ctx, up if CHAINS[chain][2] == 1 else down),
            device_id_type=MESH,
        )

    def tokens(chain):
        return slice(CHAINS[chain][3] * half, (CHAINS[chain][3] + 1) * half)

    for r in (4, 5, 3, 6, 2, 7, 1, 0):
        weight_load(r).wait()
        share_of = jnp.dot(att[...], w_ref[r], preferred_element_type=jnp.float32)
        for chain in range(4):
            if stops(chain)[0] == r:
                sums[chain, 0] = share_of[tokens(chain), :].astype(jnp.bfloat16)
        part[r] = share_of
        for chain in range(4):
            if stops(chain)[0] == r:
                send(chain, 0).start()

    for i in range(4):
        for chain in range(4):
            order = stops(chain) + [0]
            if i + 1 >= len(order):
                continue
            send(chain, i).wait_recv()
            mine = part[order[i + 1], tokens(chain), :] + landed[chain, i].astype(jnp.float32)
            if order[i + 1] == 0:
                part[0, tokens(chain), :] = mine
            else:
                sums[chain, i + 1] = mine.astype(jnp.bfloat16)
                send(chain, i + 1).start()
    out_ref[...] = jnp.transpose(part[0]).astype(jnp.bfloat16)

    for chain in range(4):
        for i in range(len(stops(chain))):
            send(chain, i).wait_send()

    for piece, slot, delta in EDGES:
        edge(piece, slot, delta).wait_send()
    for piece in range(2):
        for slot in SHARED[piece]:
            share(piece, slot).wait_send()

    @pl.when(core == 1)
    def _():
        last().wait_send()


def on_device(n_ctx, n_head, queries, key_vectors, value_vectors, out_weight, offsets):
    rows, columns = queries.shape
    depth, features = out_weight.shape
    width = features // n_head
    dma = pltpu.SemaphoreType.DMA
    return pl.pallas_call(
        functools.partial(kernel, n_ctx, n_head),
        out_shape=jax.ShapeDtypeStruct((width, rows), jnp.bfloat16),
        in_specs=[pl.BlockSpec(memory_space=pltpu.SMEM)] + [pl.BlockSpec(memory_space=pl.ANY)] * 4,
        out_specs=pl.BlockSpec(memory_space=pltpu.VMEM),
        scratch_shapes=[
            pltpu.VMEM((9, 2, 2, rows, HEAD_DIM), jnp.bfloat16),
            pltpu.VMEM((rows, columns), jnp.bfloat16),
            pltpu.VMEM((n_head, depth, width), jnp.bfloat16),
            pltpu.VMEM((16, HEAD_DIM), jnp.int32),
            pltpu.VMEM((columns // HEAD_DIM, rows, 2 * HEAD_DIM), jnp.bfloat16),
            pltpu.VMEM((8, rows), jnp.float32),
            pltpu.VMEM((columns // HEAD_DIM, HEAD_DIM + 16, rows), jnp.float32),
            pltpu.VMEM((rows, columns), jnp.bfloat16),
            pltpu.VMEM((n_head, rows, width), jnp.float32),
            pltpu.VMEM((4, 4, rows // 2, width), jnp.bfloat16),
            pltpu.VMEM((4, 4, rows // 2, width), jnp.bfloat16),
            dma((3,)),
            dma((n_head,)),
            dma((2, 9)),
            dma((2, 9)),
            dma((2, 9)),
            dma((2, 9)),
            dma((1,)),
            dma((1,)),
            dma((4, 4)),
            dma((4, 4)),
        ],
        compiler_params=pltpu.CompilerParams(
            collective_id=0, has_side_effects=True, vmem_limit_bytes=60 * 1024 * 1024
        ),
    )(offsets, queries, key_vectors, value_vectors, out_weight)


def solution(mesh):
    placed = (P("ctx", "head"), P("ctx", "head"), P("ctx", "head"), P("head", None), P())
    return jax.shard_map(
        functools.partial(on_device, mesh.shape["ctx"], mesh.shape["head"]),
        mesh=mesh,
        in_specs=placed,
        out_specs=P("head", "ctx"),
        check_vma=False,
    )
```

time: 77.9 us -> 72.7 us (0.933)
  the two profiles are of different devices: /device:TPU:8 before, /device:TPU:2 now
where the time goes in v2:
time: 72.7 us; the launch traced here: 72.5 us
  Pallas kernels  70.8 us (97%)
  local copies, waits for them, and re-layouts  1.67 us (2%)
    pallas_call x1, Pallas kernels, on_device(): pl.pallas_call(functools.partial(kernel, n_ctx, n_head), out_shape=jax.Sh...  70.8 us
    unnamed x1, local copies, waits for them, and re-layouts  1.67 us

profile of v2, /device:TPU:2, one launch (start us, length us, event | category | flops | bytes accessed | tf_op | source)
XLA Modules:
  0.0 72.5 jit_solution(5270804621911062250)
XLA Ops:
  0.0 70.8 %shard_map.55 = bf16[512,256]{1,0:T(8,128)(2,1)} custom-call(s32[25]{0:T(128)} %offsets_ref.1, bf16[256,512]{1,0:T(8,128)(2,1)} %q_hbm.1, bf16[256,128]{1,0:T(8,128)(2,1)} %k_hbm.1, bf16[256,128]{1,0:T(8,128)(2,1)} %v_hbm.1, bf16[512,4096]{1,0:T(8,128)(2,1)} %w_hbm.1), custom_call_target="tpu_custom_call" | custom-call | tf_op jit(solution)/shard_map/pallas_call | solution.py:291
  70.9 1.7 %copy.7 = bf16[512,256]{1,0:T(8,128)(2,1)} copy(bf16[512,256]{1,0:T(8,128)(2,1)} %shard_map.55) | data formatting | bytes 524288

commit v3 on v2

--- a/solution.py
+++ b/solution.py
@@ -14,11 +14,29 @@
 FAR = 1 << 24
 BARRED = -float(1 << 17)
 
+DEPTH = 12
 EDGES = (
-    (0, 0, 2), (0, 2, 2), (0, 4, 2), (0, 2, -1), (0, 4, -1), (0, 6, -1), (0, 6, 1),
-    (1, 0, 2), (1, 2, 2), (1, 2, -1), (1, 4, -1), (1, 0, 8), (1, 8, -2), (1, 6, 1), (1, 6, -1),
+    (0, 0, 8, 0xFFF),
+    (0, 0, 1, 0xFFF),
+    (0, 1, 2, 0xFFF),
+    (0, 1, 1, 0xFFF),
+    (0, 3, 1, 0xFFF),
+    (0, 6, -1, 0xFFF),
+    (0, 8, -2, 0xFFF),
+    (0, 8, -1, 0xFFF),
+    (1, 0, 8, 0xFFF),
+    (1, 0, 2, 0xFFF),
+    (1, 0, 1, 0xFFF),
+    (1, 2, 1, 0xFFF),
+    (1, 3, 2, 0xFFF),
+    (1, 3, 1, 0xFFF),
+    (1, 7, -1, 0xFFF),
+    (1, 8, -1, 0xFFF),
 )
-SHARED = (range(8), range(9))
+ORDER = (
+    (0, 1), (1, 1), (1, 2), (0, 8), (0, 3), (1, 8), (1, 3), (0, 6),
+    (0, 2), (0, 7), (1, 7), (0, 4), (1, 4), (1, 5), (0, 5), (1, 6),
+)
 
 CHAINS = ((4, 1, -1, 0), (4, -1, 1, 1), (5, 1, -1, 1), (3, -1, 1, 0))
 
@@ -31,7 +49,7 @@
 def kernel(
     n_ctx, n_head, offsets_ref, q_hbm, k_hbm, v_hbm, w_hbm, out_ref,
     kv, q_ref, w_ref, edges, qm, m_ref, acc, att, part, sums, landed,
-    in_sem, w_sem, hop_send, hop_recv, share_send, share_recv, last_send, last_recv,
+    in_sem, w_sem, hop_send, hop_recv, share_send, share_recv,
     sum_send, sum_recv,
 ):
     ctx, head = lax.axis_index("ctx"), lax.axis_index("head")
@@ -43,7 +61,6 @@
     width = w_ref.shape[2]
     scale = math.log2(math.e) / math.sqrt(HEAD_DIM)
     partner = ctx + 1 - 2 * core
-    across = lax.rem(ctx + n_ctx + 6 * core - 3, n_ctx)
     up, down = lax.rem(head + 1, n_head), lax.rem(head + n_head - 1, n_head)
 
     loads = [
@@ -62,12 +79,32 @@
         weight_load(r).start()
 
     barrier = pltpu.get_barrier_semaphore()
-    for delta in (1, -1, 2, -2, 8, -8):
-        near = lax.rem(ctx + n_ctx + 2 * delta, n_ctx)
-        pl.semaphore_signal(barrier, inc=1, device_id=(near, head), device_id_type=MESH)
-    for to in ((partner, head), (across, head), (ctx, up), (ctx, down)):
+    place = lax.rem(lax.div(ctx, 2), DEPTH)
+
+    def holds(mask, at):
+        return lax.rem(lax.shift_right_logical(jnp.int32(mask), at), 2)
+
+    def if_sends(mask, act):
+        if mask == (1 << DEPTH) - 1:
+            act()
+        else:
+            pl.when(holds(mask, place) == 1)(act)
+
+    reach = {}
+    for _, _, delta, mask in EDGES:
+        reach[delta] = reach.get(delta, 0) | mask
+    count = 3
+    for delta, mask in reach.items():
+        source = lax.rem(ctx + n_ctx - 2 * delta, n_ctx)
+        count = count + holds(mask, place)
+
+        @pl.when(holds(mask, lax.rem(lax.div(source, 2), DEPTH)) == 1)
+        def _():
+            pl.semaphore_signal(barrier, inc=1, device_id=(source, head), device_id_type=MESH)
+
+    for to in ((partner, head), (ctx, up), (ctx, down)):
         pl.semaphore_signal(barrier, inc=1, device_id=to, device_id_type=MESH)
-    pl.semaphore_wait(barrier, 10)
+    pl.semaphore_wait(barrier, count)
 
     def chip(delta):
         return lax.rem(ctx + n_ctx + 2 * delta, n_ctx)
@@ -76,7 +113,7 @@
         return pltpu.make_async_remote_copy(
             src_ref=kv.at[slot, core, piece],
             dst_ref=kv.at[slot + delta, core, piece],
-            send_sem=hop_send.at[piece, slot + delta],
+            send_sem=hop_send.at[piece, slot, slot + delta],
             recv_sem=hop_recv.at[piece, slot + delta],
             device_id=(chip(delta), head),
             device_id_type=MESH,
@@ -92,15 +129,11 @@
             device_id_type=MESH,
         )
 
-    def last():
-        return pltpu.make_async_remote_copy(
-            src_ref=kv.at[6, 1, 0],
-            dst_ref=kv.at[8, 1, 0],
-            send_sem=last_send.at[0],
-            recv_sem=last_recv.at[0],
-            device_id=(across, head),
-            device_id_type=MESH,
-        )
+    def pass_on(piece, slot):
+        for kind, at, delta, mask in EDGES:
+            if (kind, at) == (piece, slot):
+                if_sends(mask, lambda: edge(piece, slot, delta).start())
+        share(piece, slot).start()
 
     def first_of(slot, parity):
         return (ctx - core - 2 * slot + parity) * rows
@@ -141,9 +174,7 @@
 
     for piece in range(2):
         loads[piece].wait()
-        edge(piece, 0, 2).start()
-        share(piece, 0).start()
-    edge(1, 0, 8).start()
+        pass_on(piece, 0)
 
     lane = lax.broadcasted_iota(jnp.int32, (8, HEAD_DIM), 1)
     low = jnp.full((8, HEAD_DIM), FAR, jnp.int32)
@@ -173,56 +204,36 @@
         share(1, slot).wait_recv()
         block(slot, other, first_of(slot, other))
 
-    def arrived(piece, slot, *deltas):
+    def oldest():
+        share(0, 8).wait_recv()
+        share(1, 8).wait_recv()
+
+        @pl.when(core == 0)
+        def _():
+            block(8, 1, first_of(8, 1))
+
+    def first_theirs():
+        share(0, 0).wait_recv()
+        share(1, 0).wait_recv()
+        block(0, other, jnp.where(core == 0, -FAR // 2, first_of(0, other)))
+
+    block(0, core, first_of(0, core), diagonal=True)
+    due = [first_theirs]
+    here = set()
+    for piece, slot in ORDER:
         edge(piece, slot, 0).wait_recv()
-        for delta in deltas:
-            edge(piece, slot, delta).start()
-        share(piece, slot).start()
-
-    block(0, core, first_of(0, core), diagonal=True)
-    share(0, 0).wait_recv()
-    share(1, 0).wait_recv()
-    block(0, other, jnp.where(core == 0, -FAR // 2, first_of(0, other)))
-    arrived(0, 2, 2, -1)
-    arrived(1, 2, 2, -1)
-    mine(2)
-    arrived(1, 8, -2)
-    theirs(2)
-    arrived(0, 4, 2, -1)
-    arrived(1, 4, -1)
-    mine(4)
-    arrived(0, 1)
-    arrived(1, 1)
-    mine(1)
-    arrived(1, 6, 1, -1)
-    theirs(4)
-    arrived(0, 6, 1, -1)
-
-    @pl.when(core == 1)
-    def _():
-        last().start()
-
-    theirs(1)
-    mine(6)
-    arrived(0, 3)
-    arrived(1, 3)
-    mine(3)
-    theirs(6)
-    arrived(0, 5)
-    arrived(1, 5)
-    theirs(3)
-    arrived(0, 7)
-    arrived(1, 7)
-    mine(5)
-    mine(7)
-    theirs(5)
-    theirs(7)
-    share(1, 8).wait_recv()
-
-    @pl.when(core == 0)
-    def _():
-        last().wait_recv()
-        block(8, 1, first_of(8, 1))
+        pass_on(piece, slot)
+        if slot in here:
+            if due:
+                due.pop(0)()
+            if slot == 8:
+                due.append(oldest)
+            else:
+                mine(slot)
+                due.append(functools.partial(theirs, slot))
+        here.add(slot)
+    for left in due:
+        left()
 
     for h in range(heads):
         cols = slice(h * HEAD_DIM, (h + 1) * HEAD_DIM)
@@ -272,15 +283,11 @@
         for i in range(len(stops(chain))):
             send(chain, i).wait_send()
 
-    for piece, slot, delta in EDGES:
-        edge(piece, slot, delta).wait_send()
+    for piece, at, delta, mask in EDGES:
+        if_sends(mask, lambda: edge(piece, at, delta).wait_send())
     for piece in range(2):
-        for slot in SHARED[piece]:
+        for slot in range(9):
             share(piece, slot).wait_send()
-
-    @pl.when(core == 1)
-    def _():
-        last().wait_send()
 
 
 def on_device(n_ctx, n_head, queries, key_vectors, value_vectors, out_weight, offsets):
@@ -307,12 +314,10 @@
             pltpu.VMEM((4, 4, rows // 2, width), jnp.bfloat16),
             dma((3,)),
             dma((n_head,)),
+            dma((2, 9, 9)),
             dma((2, 9)),
             dma((2, 9)),
             dma((2, 9)),
-            dma((2, 9)),
-            dma((1,)),
-            dma((1,)),
             dma((4, 4)),
             dma((4, 4)),
         ],

time: 72.7 us -> 70 us (0.963)
  the two profiles are of different devices: /device:TPU:2 before, /device:TPU:1 now
where the time goes in v3:
time: 70 us; the launch traced here: 69.9 us
  Pallas kernels  68.2 us (97%)
  local copies, waits for them, and re-layouts  1.67 us (2%)
    pallas_call x1, Pallas kernels, on_device(): pl.pallas_call(functools.partial(kernel, n_ctx, n_head), out_shape=jax.Sh...  68.2 us
    unnamed x1, local copies, waits for them, and re-layouts  1.67 us

profile of v3, /device:TPU:1, one launch (start us, length us, event | category | flops | bytes accessed | tf_op | source)
XLA Modules:
  0.0 69.9 jit_solution(9361665191162503886)
XLA Ops:
  0.0 68.2 %shard_map.55 = bf16[512,256]{1,0:T(8,128)(2,1)} custom-call(s32[25]{0:T(128)} %offsets_ref.1, bf16[256,512]{1,0:T(8,128)(2,1)} %q_hbm.1, bf16[256,128]{1,0:T(8,128)(2,1)} %k_hbm.1, bf16[256,128]{1,0:T(8,128)(2,1)} %v_hbm.1, bf16[512,4096]{1,0:T(8,128)(2,1)} %w_hbm.1), custom_call_target="tpu_custom_call" | custom-call | tf_op jit(solution)/shard_map/pallas_call | solution.py:298
  68.2 1.7 %copy.7 = bf16[512,256]{1,0:T(8,128)(2,1)} copy(bf16[512,256]{1,0:T(8,128)(2,1)} %shard_map.55) | data formatting | bytes 524288

commit v4 on v3

--- a/solution.py
+++ b/solution.py
@@ -138,17 +138,21 @@
     def first_of(slot, parity):
         return (ctx - core - 2 * slot + parity) * rows
 
-    def block(slot, parity, first, diagonal=False):
-        keys = kv[slot, parity, 0]
-        values = jnp.transpose(kv[slot, parity, 1])
-        at = first + lax.broadcasted_iota(jnp.int32, (rows, HEAD_DIM), 0)
-        among = (at >= edges[0:1, :]) & (at < edges[8:9, :])
-        keys = jnp.concatenate([keys, jnp.where(among, 1.0, 0.0).astype(jnp.bfloat16)], axis=1)
-        values = jnp.concatenate([values, jnp.ones((16, rows), jnp.bfloat16)], axis=0)
+    def blocks(group, diagonal=False):
+        keys, values = [], []
+        for slot, parity, first in group:
+            at = first + lax.broadcasted_iota(jnp.int32, (rows, HEAD_DIM), 0)
+            among = (at >= edges[0:1, :]) & (at < edges[8:9, :])
+            named = jnp.where(among, 1.0, 0.0).astype(jnp.bfloat16)
+            keys.append(jnp.concatenate([kv[slot, parity, 0], named], axis=1))
+            values.append(jnp.transpose(kv[slot, parity, 1]))
+        keys = jnp.concatenate(keys, axis=0)
+        values = jnp.concatenate(values, axis=1)
+        values = jnp.concatenate([values, jnp.ones((16, keys.shape[0]), jnp.bfloat16)], axis=0)
         if diagonal:
-            seen = lax.broadcasted_iota(jnp.int32, (rows, rows), 0) <= lax.broadcasted_iota(
-                jnp.int32, (rows, rows), 1
-            )
+            key_at = lax.broadcasted_iota(jnp.int32, (keys.shape[0], rows), 0)
+            query_at = lax.broadcasted_iota(jnp.int32, (keys.shape[0], rows), 1)
+            seen = (key_at >= rows) | (key_at <= query_at)
 
         def score(h):
             got = lax.dot_general(
@@ -196,44 +200,38 @@
         qm[h, :, 0:HEAD_DIM] = q_ref[:, h * HEAD_DIM : (h + 1) * HEAD_DIM]
         qm[h, :, HEAD_DIM : 2 * HEAD_DIM] = barred
 
-    def mine(slot):
-        block(slot, core, first_of(slot, core))
-
-    def theirs(slot):
+    def shared(slot):
         share(0, slot).wait_recv()
         share(1, slot).wait_recv()
-        block(slot, other, first_of(slot, other))
-
-    def oldest():
-        share(0, 8).wait_recv()
-        share(1, 8).wait_recv()
-
-        @pl.when(core == 0)
-        def _():
-            block(8, 1, first_of(8, 1))
-
-    def first_theirs():
-        share(0, 0).wait_recv()
-        share(1, 0).wait_recv()
-        block(0, other, jnp.where(core == 0, -FAR // 2, first_of(0, other)))
-
-    block(0, core, first_of(0, core), diagonal=True)
-    due = [first_theirs]
+
+    def theirs(slot):
+        shared(slot)
+        return (slot, other, first_of(slot, other))
+
+    blocks([(0, core, first_of(0, core))], diagonal=True)
+    shared(0)
+    due = [(0, other, jnp.where(core == 0, -FAR // 2, first_of(0, other)))]
+    waiting = []
     here = set()
     for piece, slot in ORDER:
         edge(piece, slot, 0).wait_recv()
         pass_on(piece, slot)
-        if slot in here:
-            if due:
-                due.pop(0)()
-            if slot == 8:
-                due.append(oldest)
-            else:
-                mine(slot)
-                due.append(functools.partial(theirs, slot))
+        if slot in here and slot != 8:
+            if not due:
+                due.append(theirs(waiting.pop(0)))
+            blocks([due.pop(0), (slot, core, first_of(slot, core))])
+            waiting.append(slot)
         here.add(slot)
-    for left in due:
-        left()
+    while waiting:
+        due.append(theirs(waiting.pop(0)))
+        if len(due) == 2 or not waiting:
+            blocks(due)
+            due = []
+    shared(8)
+
+    @pl.when(core == 0)
+    def _():
+        blocks([(8, 1, first_of(8, 1))])
 
     for h in range(heads):
         cols = slice(h * HEAD_DIM, (h + 1) * HEAD_DIM)

time: 70 us -> 68.4 us (0.977)
  Pallas kernels: 68.2 us -> 66.5 us
    pallas_call x1, Pallas kernels: 68.2 us -> 66.5 us  [on_device(): pl.pallas_call(functools.partial(kernel, n_ctx, n_head), out_shape=jax.Sh...]
where the time goes in v4:
time: 68.4 us; the launch traced here: 68.2 us
  Pallas kernels  66.5 us (97%)
  local copies, waits for them, and re-layouts  1.67 us (2%)
    pallas_call x1, Pallas kernels, on_device(): pl.pallas_call(functools.partial(kernel, n_ctx, n_head), out_shape=jax.Sh...  66.5 us
    unnamed x1, local copies, waits for them, and re-layouts  1.67 us

profile of v4, /device:TPU:1, one launch (start us, length us, event | category | flops | bytes accessed | tf_op | source)
XLA Modules:
  0.0 68.2 jit_solution(14625622151028631337)
XLA Ops:
  0.0 66.5 %shard_map.55 = bf16[512,256]{1,0:T(8,128)(2,1)} custom-call(s32[25]{0:T(128)} %offsets_ref.1, bf16[256,512]{1,0:T(8,128)(2,1)} %q_hbm.1, bf16[256,128]{1,0:T(8,128)(2,1)} %k_hbm.1, bf16[256,128]{1,0:T(8,128)(2,1)} %v_hbm.1, bf16[512,4096]{1,0:T(8,128)(2,1)} %w_hbm.1), custom_call_target="tpu_custom_call" | custom-call | tf_op jit(solution)/shard_map/pallas_call | solution.py:296
  66.5 1.7 %copy.7 = bf16[512,256]{1,0:T(8,128)(2,1)} copy(bf16[512,256]{1,0:T(8,128)(2,1)} %shard_map.55) | data formatting | bytes 524288

commit v5 on v4

--- a/solution.py
+++ b/solution.py
@@ -38,7 +38,10 @@
     (0, 2), (0, 7), (1, 7), (0, 4), (1, 4), (1, 5), (0, 5), (1, 6),
 )
 
-CHAINS = ((4, 1, -1, 0), (4, -1, 1, 1), (5, 1, -1, 1), (3, -1, 1, 0))
+CHAINS = (
+    (4, 1, -1, 0), (4, -1, 1, 2), (4, 1, -1, 1), (4, -1, 1, 3),
+    (5, 1, -1, 2), (3, -1, 1, 0), (5, 1, -1, 3), (3, -1, 1, 1),
+)
 
 
 def stops(chain):
@@ -57,7 +60,7 @@
     other = 1 - core
     rows = q_ref.shape[0]
     heads = q_ref.shape[1] // HEAD_DIM
-    half = rows // 2
+    part_rows = rows // 4
     width = w_ref.shape[2]
     scale = math.log2(math.e) / math.sqrt(HEAD_DIM)
     partner = ctx + 1 - 2 * core
@@ -250,21 +253,21 @@
         )
 
     def tokens(chain):
-        return slice(CHAINS[chain][3] * half, (CHAINS[chain][3] + 1) * half)
+        return slice(CHAINS[chain][3] * part_rows, (CHAINS[chain][3] + 1) * part_rows)
 
     for r in (4, 5, 3, 6, 2, 7, 1, 0):
         weight_load(r).wait()
         share_of = jnp.dot(att[...], w_ref[r], preferred_element_type=jnp.float32)
-        for chain in range(4):
+        for chain in range(len(CHAINS)):
             if stops(chain)[0] == r:
                 sums[chain, 0] = share_of[tokens(chain), :].astype(jnp.bfloat16)
         part[r] = share_of
-        for chain in range(4):
+        for chain in range(len(CHAINS)):
             if stops(chain)[0] == r:
                 send(chain, 0).start()
 
     for i in range(4):
-        for chain in range(4):
+        for chain in range(len(CHAINS)):
             order = stops(chain) + [0]
             if i + 1 >= len(order):
                 continue
@@ -277,7 +280,7 @@
                 send(chain, i + 1).start()
     out_ref[...] = jnp.transpose(part[0]).astype(jnp.bfloat16)
 
-    for chain in range(4):
+    for chain in range(len(CHAINS)):
         for i in range(len(stops(chain))):
             send(chain, i).wait_send()
 
@@ -308,16 +311,16 @@
             pltpu.VMEM((columns // HEAD_DIM, HEAD_DIM + 16, rows), jnp.float32),
             pltpu.VMEM((rows, columns), jnp.bfloat16),
             pltpu.VMEM((n_head, rows, width), jnp.float32),
-            pltpu.VMEM((4, 4, rows // 2, width), jnp.bfloat16),
-            pltpu.VMEM((4, 4, rows // 2, width), jnp.bfloat16),
+            pltpu.VMEM((len(CHAINS), 4, rows // 4, width), jnp.bfloat16),
+            pltpu.VMEM((len(CHAINS), 4, rows // 4, width), jnp.bfloat16),
             dma((3,)),
             dma((n_head,)),
             dma((2, 9, 9)),
             dma((2, 9)),
             dma((2, 9)),
             dma((2, 9)),
-            dma((4, 4)),
-            dma((4, 4)),
+            dma((len(CHAINS), 4)),
+            dma((len(CHAINS), 4)),
         ],
         compiler_params=pltpu.CompilerParams(
             collective_id=0, has_side_effects=True, vmem_limit_bytes=60 * 1024 * 1024

time: 68.4 us -> 69.2 us (1.012)
  Pallas kernels: 66.5 us -> 67.3 us
    pallas_call x1, Pallas kernels: 66.5 us -> 67.3 us  [on_device(): pl.pallas_call(functools.partial(kernel, n_ctx, n_head), out_shape=jax.Sh...]
where the time goes in v5:
time: 69.2 us; the launch traced here: 69 us
  Pallas kernels  67.3 us (97%)
  local copies, waits for them, and re-layouts  1.67 us (2%)
    pallas_call x1, Pallas kernels, on_device(): pl.pallas_call(functools.partial(kernel, n_ctx, n_head), out_shape=jax.Sh...  67.3 us
    unnamed x1, local copies, waits for them, and re-layouts  1.67 us

profile of v5, /device:TPU:1, one launch (start us, length us, event | category | flops | bytes accessed | tf_op | source)
XLA Modules:
  0.0 69.0 jit_solution(10983263094391725271)
XLA Ops:
  0.0 67.3 %shard_map.55 = bf16[512,256]{1,0:T(8,128)(2,1)} custom-call(s32[25]{0:T(128)} %offsets_ref.1, bf16[256,512]{1,0:T(8,128)(2,1)} %q_hbm.1, bf16[256,128]{1,0:T(8,128)(2,1)} %k_hbm.1, bf16[256,128]{1,0:T(8,128)(2,1)} %v_hbm.1, bf16[512,4096]{1,0:T(8,128)(2,1)} %w_hbm.1), custom_call_target="tpu_custom_call" | custom-call | tf_op jit(solution)/shard_map/pallas_call | solution.py:299
  67.3 1.7 %copy.7 = bf16[512,256]{1,0:T(8,128)(2,1)} copy(bf16[512,256]{1,0:T(8,128)(2,1)} %shard_map.55) | data formatting | bytes 524288
